TPU v7x, 256 devices: a whole 4x4x8 slice. The times are simulated.
256 devices in a mesh: dp: 4 (over y), sx: 4 (over x_lo, core), sy: 16 (over z, x_hi).
Axes of the slice: x: 4 (x_hi: 2, x_lo: 2; x = x_hi * 2 + x_lo), y: 4, z: 8, core: 2. Of those that a mesh axis runs over, the one named last changes fastest.
Arguments:
- features: bfloat16 [4, 4, 16, 3072, 128], P('dp', 'sx', 'sy'), may hold values from -6 to 6
- cotangent: bfloat16 [4, 4, 16, 3072, 128], P('dp', 'sx', 'sy'), may hold values from -6 to 6
- weights: bfloat16 [27, 128, 128], replicated, may hold values from -0.109375 to 0.109375
- tables: int32 [4, 4, 16, 27, 24], P('dp', 'sx', 'sy'), may hold values from 0 to 56, as said below
- send_lists: int32 [4, 4, 16, 4], P('dp', 'sx', 'sy'), may hold values from 0 to 23, as said below
- counts: int32 [4, 4, 16], P('dp', 'sx', 'sy'), may hold values from 6 to 24, as said below
Outputs:
- output: bfloat16 [4, 4, 16, 3072, 128], P('dp', 'sx', 'sy')
- input_grad: bfloat16 [4, 4, 16, 3072, 128], P('dp', 'sx', 'sy')
- weight_grad: float32 [27, 128, 128], replicated
Inputs may be any that keep to these rules, and one draw needn't show every extreme that they name: `tables`: entries below 24 name a block of the tile, 24 + n * 4 + s' the s'-th sent block of neighbour direction n, 56 the empty block; under offset 27 // 2 every block reads itself. `send_lists`: the 4 blocks of one tile are distinct. `counts`: some tile has all 24 blocks active.
All inputs are finite; a program needn't handle non-finite values.
Results may differ from a plain program's by a relative error of at most 0.001.
Values may be sent and summed in bfloat16 or wider, within the bound.
A program may use at most 64 MiB of HBM per device.

v0:
```python
import math
import jax
import jax.numpy as jnp
from jax import lax
from jax.sharding import PartitionSpec as P

directions = ((-1, -1), (-1, 0), (-1, 1), (0, -1), (0, 1), (1, -1), (1, 0), (1, 1))


def shifted(block, axis, distance):
    devices = range(lax.axis_size(axis))
    route = [(i - distance, i) for i in devices if i - distance in devices]
    return lax.ppermute(block, axis, route)


def padded(cells, sides, width):
    for axis, dim in sides:
        count = lax.axis_size(axis)
        ends = count - 1
        head = lax.slice_in_dim(cells, 0, width, axis=dim)
        tail = lax.slice_in_dim(cells, cells.shape[dim] - width, cells.shape[dim], axis=dim)
        cells = jnp.concatenate(
            [
                lax.ppermute(tail, axis, [(i, (i + 1) % count) for i in range(ends)]),
                cells,
                lax.ppermute(head, axis, [((i + 1) % count, i) for i in range(ends)]),
            ],
            axis=dim,
        )
    return cells


def local(features, cotangent, weights, tables, send_lists, counts):
    num_blocks = tables.shape[4]
    num_sent = send_lists.shape[3]
    offsets = weights.shape[0]
    channels = weights.shape[1]
    width_block = features.shape[3] // num_blocks
    group_size = 4
    active = (jnp.arange(num_blocks) < counts.reshape(())).astype(jnp.bfloat16)[:, None, None]
    active_full = active.astype(jnp.float32)
    blocks_in = features.reshape(num_blocks, width_block, channels) * active
    blocks_grad = cotangent.reshape(num_blocks, width_block, channels) * active
    offset_table = tables.reshape(offsets, num_blocks)
    sent_ids = send_lists.reshape(num_sent)
    groups = jnp.arange(num_blocks // group_size)

    def grad_group(accum, group):
        start = group * group_size
        picks = lax.dynamic_slice_in_dim(offset_table, start, group_size, 1)
        grad_rows = lax.dynamic_slice_in_dim(blocks_grad, start, group_size, 0)
        contrib = jnp.einsum(
            "gvd,kcd->kgvc", grad_rows, weights, preferred_element_type=jnp.float32
        )
        accum = accum.at[picks.reshape(-1)].add(
            contrib.reshape(offsets * group_size, width_block, channels)
        )
        return (accum, None)

    num_ext = num_blocks + 8 * num_sent + 1
    grad_ext, unused_rows = lax.scan(
        grad_group, jnp.zeros((num_ext, width_block, channels), jnp.float32), groups
    )
    halo_grads = grad_ext[num_blocks : num_blocks + 8 * num_sent].reshape(
        8, num_sent * width_block, channels
    )
    received = jnp.zeros((num_sent * width_block, channels), jnp.float32)
    for slot_index, (step_x, step_y) in enumerate(directions):
        portion = halo_grads[slot_index]
        if step_x != 0:
            portion = shifted(portion, "sx", step_x)
        if step_y != 0:
            portion = shifted(portion, "sy", step_y)
        received = received + portion
    local_grad = (
        grad_ext[:num_blocks].at[sent_ids].add(received.reshape(num_sent, width_block, channels))
    )
    input_grad = (local_grad * active_full).astype(jnp.bfloat16).reshape(features.shape)
    outgoing = blocks_in[sent_ids].reshape(1, 1, num_sent * width_block, channels)
    bordered = padded(outgoing, (("sx", 0), ("sy", 1)), 1)
    neighbours = [
        bordered[1 + step_x, 1 + step_y].reshape(num_sent, width_block, channels)
        for step_x, step_y in directions
    ]
    extended = jnp.concatenate(
        [blocks_in] + neighbours + [jnp.zeros((1, width_block, channels), jnp.bfloat16)], axis=0
    )

    def forward_group(accum, group):
        start = group * group_size
        picks = lax.dynamic_slice_in_dim(offset_table, start, group_size, 1)
        gathered = extended[picks]
        grad_rows = lax.dynamic_slice_in_dim(blocks_grad, start, group_size, 0)
        rows_active = lax.dynamic_slice_in_dim(active_full, start, group_size, 0)
        outputs = jnp.einsum("kgvc,kcd->gvd", gathered, weights, preferred_element_type=jnp.float32)
        accum = accum + jnp.einsum(
            "kgvc,gvd->kcd", gathered, grad_rows, preferred_element_type=jnp.float32
        )
        return (accum, (outputs * rows_active).astype(jnp.bfloat16))

    weight_part, outputs = lax.scan(
        forward_group, jnp.zeros((offsets, channels, channels), jnp.float32), groups
    )
    output = outputs.reshape(features.shape)
    total = (
        num_blocks * width_block * lax.axis_size("dp") * lax.axis_size("sx") * lax.axis_size("sy")
    )
    scaled_part = weight_part * (1.0 / math.sqrt(total))
    weight_grad = lax.psum(scaled_part, ("dp", "sx", "sy"))
    return (output, input_grad, weight_grad)


def solution(mesh):
    return jax.shard_map(
        local,
        mesh=mesh,
        in_specs=(
            P("dp", "sx", "sy", None, None),
            P("dp", "sx", "sy", None, None),
            P(),
            P("dp", "sx", "sy", None, None),
            P("dp", "sx", "sy", None),
            P("dp", "sx", "sy"),
        ),
        out_specs=(P("dp", "sx", "sy", None, None), P("dp", "sx", "sy", None, None), P()),
        check_vma=False,
    )
```

profile of v0, /device:TPU:2, one launch (start us, length us, event | category | flops | bytes accessed | tf_op | source)
XLA Modules:
  0.0 617.5 jit_solution(9292657915912878841)
XLA Ops:
  8.5 3.2 constant_dynamic-update-slice_fusion.9
  12.3 1.9 collective-permute-start.1
  14.3 2.4 collective-permute-start
  17.4 2.4 broadcast_in_dim.26
  19.8 184.4 %while.23 = (s32[]{:T(128)}, f32[57,128,128]{2,1,0:T(8,128)}, s32[6]{0:T(128)S(1)}, s32[27,24]{1,0:T(8,128)}, bf16[24,128,128]{2,1,0:T(8,128)(2,1)}, /*index=5*/...) while((s32[]{:T(128)}, f32[57,128,128]{2,1,0:T(8,128)}, s32[6]{0:T(128)S(1)}, ...), condition=%wide.region_4.5_spmd, body=%wide.region_2.0_spmd.sunk | while | flops 454754624 | bytes 43486336 | solution.py:61
  21.9 2.3 convolution_bitcast_fusion.3
  24.3 3.3 copy.22
  27.6 22.9 %scatter_fusion = f32[57,128,128]{2,1,0:T(8,128)} fusion(f32[57,128,128]{2,1,0:T(8,128)} %get-tuple-element.307, s32[108]{0:T(128)S(1)} %fusion.33, f32[108,128,128]{2,1,0:T(8,128)} %bitcast.107), kind=kCustom, calls=%fused_computation.2.clone.1 | custom fusion | flops 1769472 | bytes 21234096 | tf_op jit(solution)/shard_map/while/body/eval_jaxpr/scatter-add | solution.py:55
  52.6 2.3 convolution_bitcast_fusion.3
  55.0 3.3 copy.22
  58.3 22.9 %scatter_fusion = f32[57,128,128]{2,1,0:T(8,128)} fusion(f32[57,128,128]{2,1,0:T(8,128)} %get-tuple-element.307, s32[108]{0:T(128)S(1)} %fusion.33, f32[108,128,128]{2,1,0:T(8,128)} %bitcast.107), kind=kCustom, calls=%fused_computation.2.clone.1 | custom fusion | flops 1769472 | bytes 21234096 | tf_op jit(solution)/shard_map/while/body/eval_jaxpr/scatter-add | solution.py:55
  83.4 2.3 convolution_bitcast_fusion.3
  85.7 3.3 copy.22
  89.1 22.8 %scatter_fusion = f32[57,128,128]{2,1,0:T(8,128)} fusion(f32[57,128,128]{2,1,0:T(8,128)} %get-tuple-element.307, s32[108]{0:T(128)S(1)} %fusion.33, f32[108,128,128]{2,1,0:T(8,128)} %bitcast.107), kind=kCustom, calls=%fused_computation.2.clone.1 | custom fusion | flops 1769472 | bytes 21234096 | tf_op jit(solution)/shard_map/while/body/eval_jaxpr/scatter-add | solution.py:55
  114.0 2.3 convolution_bitcast_fusion.3
  116.4 3.3 copy.22
  119.7 23.0 %scatter_fusion = f32[57,128,128]{2,1,0:T(8,128)} fusion(f32[57,128,128]{2,1,0:T(8,128)} %get-tuple-element.307, s32[108]{0:T(128)S(1)} %fusion.33, f32[108,128,128]{2,1,0:T(8,128)} %bitcast.107), kind=kCustom, calls=%fused_computation.2.clone.1 | custom fusion | flops 1769472 | bytes 21234096 | tf_op jit(solution)/shard_map/while/body/eval_jaxpr/scatter-add | solution.py:55
  144.9 2.3 convolution_bitcast_fusion.3
  147.2 3.3 copy.22
  150.6 22.9 %scatter_fusion = f32[57,128,128]{2,1,0:T(8,128)} fusion(f32[57,128,128]{2,1,0:T(8,128)} %get-tuple-element.307, s32[108]{0:T(128)S(1)} %fusion.33, f32[108,128,128]{2,1,0:T(8,128)} %bitcast.107), kind=kCustom, calls=%fused_computation.2.clone.1 | custom fusion | flops 1769472 | bytes 21234096 | tf_op jit(solution)/shard_map/while/body/eval_jaxpr/scatter-add | solution.py:55
  175.6 2.3 convolution_bitcast_fusion.3
  177.9 3.3 copy.22
  181.3 22.9 %scatter_fusion = f32[57,128,128]{2,1,0:T(8,128)} fusion(f32[57,128,128]{2,1,0:T(8,128)} %get-tuple-element.307, s32[108]{0:T(128)S(1)} %fusion.33, f32[108,128,128]{2,1,0:T(8,128)} %bitcast.107), kind=kCustom, calls=%fused_computation.2.clone.1 | custom fusion | flops 1769472 | bytes 21234096 | tf_op jit(solution)/shard_map/while/body/eval_jaxpr/scatter-add | solution.py:55
  204.3 4.3 collective-permute-start.2
  208.6 2.9 fusion.17
  211.4 1.9 collective-permute-start.14
  213.4 3.6 collective-permute-start.6
  217.0 1.9 collective-permute-start.13
  218.9 1.9 collective-permute-start.11
  220.9 1.3 collective-permute-start.3
  223.6 10.0 %collective-permute-done.3 = bf16[3,1,512,128]{3,2,1,0:T(8,128)(2,1)S(1)} collective-permute-done((bf16[3,1,512,128]{3,2,1,0:T(8,128)(2,1)S(1)}, bf16[3,1,512,128]{3,2,1,0:T(8,128)(2,1)S(1)}, u32[]{:S(2)}, u32[]{:S(2)}) %collective-permute-start.3) | collective-permute-done | bytes 393248 | tf_op jit(solution)/shard_map/ppermute | solution.py:26
  233.5 6.1 collective-permute-start.10
  244.8 79.9 %while.24 = (s32[]{:T(128)}, f32[27,128,128]{2,1,0:T(8,128)}, bf16[6,4,128,128]{3,2,1,0:T(8,128)(2,1)}, s32[6]{0:T(128)}, s32[27,24]{1,0:T(8,128)}, /*index=5*/b...) while((s32[]{:T(128)}, f32[27,128,128]{2,1,0:T(8,128)}, ...), condition=%wide.region_1.0_spmd.clone, body=%wide.region_0.1_spmd.clone.sunk | while | flops 906986816 | bytes 33004880 | solution.py:101
  248.2 2.7 gather_fusion
  251.0 3.0 fusion.39
  254.0 2.9 bitcast_add_fusion.2
  261.5 2.7 gather_fusion
  264.3 3.0 fusion.39
  267.3 2.9 bitcast_add_fusion.2
  274.8 2.7 gather_fusion
  277.6 3.0 fusion.39
  280.6 2.9 bitcast_add_fusion.2
  288.1 2.7 gather_fusion
  290.9 3.0 fusion.39
  294.0 2.9 bitcast_add_fusion.2
  301.5 2.7 gather_fusion
  304.2 3.0 fusion.39
  307.3 2.9 bitcast_add_fusion.2
  314.8 2.7 gather_fusion
  317.5 3.0 fusion.39
  320.6 2.9 bitcast_add_fusion.2
  324.7 4.2 collective-permute-start.7
  328.9 4.3 collective-permute-start.4
  333.2 3.0 broadcast_multiply_fusion
  336.2 1.3 collective-permute-start.9
  337.5 6.1 collective-permute-start.15
  343.6 1.3 collective-permute-start.12
  344.9 6.1 collective-permute-start.8
  351.0 1.3 collective-permute-start.5
  352.3 1.5 slice.68
  353.8 9.3 %collective-permute-done.15 = f32[512,128]{1,0:T(8,128)S(1)} collective-permute-done((f32[512,128]{1,0:T(8,128)}, f32[512,128]{1,0:T(8,128)S(1)}, u32[]{:S(2)}, u32[]{:S(2)}) %collective-permute-start.15) | collective-permute-done | bytes 262176 | tf_op jit(solution)/shard_map/ppermute | solution.py:13
  363.1 5.7 collective-permute-done.8
  371.9 235.9 %all-reduce.2.cloned.1.call-done = f32[27,128,128]{2,1,0:T(8,128)} async-done(((f32[27,128,128]{2,1,0:T(8,128)}), f32[27,128,128]{2,1,0:T(8,128)}) %all-reduce.2.cloned.1.call-update) | async-done | bytes 1769488 | tf_op jit(solution)/shard_map/psum | solution.py:109
  607.8 2.9 copy.52
  (122 shorter events, 44.4 us)
Async XLA Ops:
  7.2 600.6 %all-reduce.2.cloned.1.call-start = ((), (), s32[]{:S(2)}) async-start(), calls=%async_computation | async-start | bytes 3538944 | tf_op jit(solution)/shard_map/psum | solution.py:109
  8.5 8.2 %copy-start.3 = (s32[1,1,1,27,24]{3,4,2,1,0:T(8,128)S(1)}, s32[1,1,1,27,24]{3,4,2,1,0:T(8,128)}, u32[]{:S(2)}) copy-start(s32[1,1,1,27,24]{3,4,2,1,0:T(8,128)} %param.13) | copy-start | bytes 7780
  12.3 191.9 %collective-permute-start.1 = (bf16[1,1,512,128]{3,2,1,0:T(8,128)(2,1)S(1)}, bf16[1,1,512,128]{3,2,1,0:T(8,128)(2,1)S(1)}, u32[]{:S(2)}, u32[]{:S(2)}) collective-permute-start(bf16[1,1,512,128]{3,2,1,0:T(8,128)(2,1)S(1)} %bitcast.116), channel_id=1, source_target_pairs={{16,0},{32,16},{48,32},{17,1},{33,17},{49,33},{18,2},{34,18},{50,3... | collective-permute-start | bytes 393224 | tf_op jit(solution)/shard_map/ppermute | solution.py:26
  14.3 189.9 %collective-permute-start = (bf16[1,1,512,128]{3,2,1,0:T(8,128)(2,1)S(1)}, bf16[1,1,512,128]{3,2,1,0:T(8,128)(2,1)S(1)}, u32[]{:S(2)}, u32[]{:S(2)}) collective-permute-start(bf16[1,1,512,128]{3,2,1,0:T(8,128)(2,1)S(1)} %bitcast.117), channel_id=1, source_target_pairs={{0,16},{16,32},{32,48},{1,17},{17,33},{33,49},{2,18},{18,34},{34,5... | collective-permute-start | bytes 393224 | tf_op jit(solution)/shard_map/ppermute | solution.py:24
  204.3 16.7 %collective-permute-start.2 = (bf16[3,1,512,128]{3,2,1,0:T(8,128)(2,1)S(1)}, bf16[3,1,512,128]{3,2,1,0:T(8,128)(2,1)S(1)}, u32[]{:S(2)}, u32[]{:S(2)}) collective-permute-start(bf16[3,1,512,128]{3,2,1,0:T(8,128)(2,1)S(1)} %pad_maximum_fusion), channel_id=1, source_target_pairs={{0,1},{1,2},{2,3},{3,4},{4,5},{5,6},{6,7},{7,8},{8,9},{9,10},{10,1... | collective-permute-start | bytes 1179656 | tf_op jit(solution)/shard_map/ppermute | solution.py:24
  211.4 113.2 %collective-permute-start.14 = (f32[512,128]{1,0:T(8,128)}, f32[512,128]{1,0:T(8,128)}, u32[]{:S(2)}, u32[]{:S(2)}) collective-permute-start(f32[512,128]{1,0:T(8,128)} %bitcast.30), channel_id=1, source_target_pairs={{0,16},{16,32},{32,48},{1,17},{17,33},{33,49},{2,18},{18,34},{34,5... | collective-permute-start | bytes 786440 | tf_op jit(solution)/shard_map/ppermute | solution.py:13
  213.4 115.5 %collective-permute-start.6 = (f32[512,128]{1,0:T(8,128)}, f32[512,128]{1,0:T(8,128)}, u32[]{:S(2)}, u32[]{:S(2)}) collective-permute-start(f32[512,128]{1,0:T(8,128)} %bitcast.24), channel_id=1, source_target_pairs={{16,0},{32,16},{48,32},{17,1},{33,17},{49,33},{18,2},{34,18},{50,3... | collective-permute-start | bytes 786440 | tf_op jit(solution)/shard_map/ppermute | solution.py:13
  217.0 119.1 %collective-permute-start.13 = (f32[512,128]{1,0:T(8,128)}, f32[512,128]{1,0:T(8,128)}, u32[]{:S(2)}, u32[]{:S(2)}) collective-permute-start(f32[512,128]{1,0:T(8,128)} %bitcast.29), channel_id=1, source_target_pairs={{0,16},{16,32},{32,48},{1,17},{17,33},{33,49},{2,18},{18,34},{34,5... | collective-permute-start | bytes 786440 | tf_op jit(solution)/shard_map/ppermute | solution.py:13
  218.9 118.5 %collective-permute-start.11 = (f32[512,128]{1,0:T(8,128)}, f32[512,128]{1,0:T(8,128)}, u32[]{:S(2)}, u32[]{:S(2)}) collective-permute-start(f32[512,128]{1,0:T(8,128)} %bitcast.28), channel_id=1, source_target_pairs={{0,16},{16,32},{32,48},{1,17},{17,33},{33,49},{2,18},{18,34},{34,5... | collective-permute-start | bytes 786440 | tf_op jit(solution)/shard_map/ppermute | solution.py:13
  220.9 12.6 %collective-permute-start.3 = (bf16[3,1,512,128]{3,2,1,0:T(8,128)(2,1)S(1)}, bf16[3,1,512,128]{3,2,1,0:T(8,128)(2,1)S(1)}, u32[]{:S(2)}, u32[]{:S(2)}) collective-permute-start(bf16[3,1,512,128]{3,2,1,0:T(8,128)(2,1)S(1)} %pad_maximum_fusion), channel_id=1, source_target_pairs={{1,0},{2,1},{3,2},{4,3},{5,4},{6,5},{7,6},{8,7},{9,8},{10,9},{11,1... | collective-permute-start | bytes 1179656 | tf_op jit(solution)/shard_map/ppermute | solution.py:26
  233.5 110.0 %collective-permute-start.10 = (f32[512,128]{1,0:T(8,128)}, f32[512,128]{1,0:T(8,128)}, u32[]{:S(2)}, u32[]{:S(2)}) collective-permute-start(f32[512,128]{1,0:T(8,128)} %bitcast.27), channel_id=1, source_target_pairs={{0,1},{1,2},{2,3},{3,4},{4,5},{5,6},{6,7},{7,8},{8,9},{9,10},{10,1... | collective-permute-start | bytes 786440 | tf_op jit(solution)/shard_map/ppermute | solution.py:13
  250.9 3.1 copy-start
  256.9 1.2 copy-start.1
  264.3 3.1 copy-start
  270.2 1.2 copy-start.1
  277.6 3.1 copy-start
  283.5 1.2 copy-start.1
  290.9 3.1 copy-start
  296.8 1.2 copy-start.1
  304.2 3.1 copy-start
  310.2 1.2 copy-start.1
  317.5 3.1 copy-start
  323.5 1.2 copy-start.1
  324.7 20.2 %collective-permute-start.7 = (f32[512,128]{1,0:T(8,128)}, f32[512,128]{1,0:T(8,128)S(1)}, u32[]{:S(2)}, u32[]{:S(2)}) collective-permute-start(f32[512,128]{1,0:T(8,128)} %bitcast.127), channel_id=1, source_target_pairs={{16,0},{32,16},{48,32},{17,1},{33,17},{49,33},{18,2},{34,18},{50,3... | collective-permute-start | bytes 786440 | tf_op jit(solution)/shard_map/ppermute | solution.py:13
  328.9 22.1 %collective-permute-start.4 = (f32[512,128]{1,0:T(8,128)}, f32[512,128]{1,0:T(8,128)S(1)}, u32[]{:S(2)}, u32[]{:S(2)}) collective-permute-start(f32[512,128]{1,0:T(8,128)} %bitcast.126), channel_id=1, source_target_pairs={{16,0},{32,16},{48,32},{17,1},{33,17},{49,33},{18,2},{34,18},{50,3... | collective-permute-start | bytes 786440 | tf_op jit(solution)/shard_map/ppermute | solution.py:13
  333.2 3.0 copy-start.2
  336.2 17.6 %collective-permute-start.9 = (f32[512,128]{1,0:T(8,128)S(1)}, f32[512,128]{1,0:T(8,128)S(1)}, u32[]{:S(2)}, u32[]{:S(2)}) collective-permute-start(f32[512,128]{1,0:T(8,128)S(1)} %bitcast.125), channel_id=1, source_target_pairs={{1,0},{2,1},{3,2},{4,3},{5,4},{6,5},{7,6},{8,7},{9,8},{10,9},{11,1... | collective-permute-start | bytes 786440 | tf_op jit(solution)/shard_map/ppermute | solution.py:13
  337.5 25.6 %collective-permute-start.15 = (f32[512,128]{1,0:T(8,128)}, f32[512,128]{1,0:T(8,128)S(1)}, u32[]{:S(2)}, u32[]{:S(2)}) collective-permute-start(f32[512,128]{1,0:T(8,128)} %collective-permute-done.14), channel_id=1, source_target_pairs={{0,1},{1,2},{2,3},{3,4},{4,5},{5,6},{6,7},{7,8},{8,9},{9,10},{10,1... | collective-permute-start | bytes 786440 | tf_op jit(solution)/shard_map/ppermute | solution.py:13
  343.6 19.5 %collective-permute-start.12 = (f32[512,128]{1,0:T(8,128)}, f32[512,128]{1,0:T(8,128)S(1)}, u32[]{:S(2)}, u32[]{:S(2)}) collective-permute-start(f32[512,128]{1,0:T(8,128)} %collective-permute-done.11), channel_id=1, source_target_pairs={{1,0},{2,1},{3,2},{4,3},{5,4},{6,5},{7,6},{8,7},{9,8},{10,9},{11,1... | collective-permute-start | bytes 786440 | tf_op jit(solution)/shard_map/ppermute | solution.py:13
  344.9 23.9 %collective-permute-start.8 = (f32[512,128]{1,0:T(8,128)S(1)}, f32[512,128]{1,0:T(8,128)S(1)}, u32[]{:S(2)}, u32[]{:S(2)}) collective-permute-start(f32[512,128]{1,0:T(8,128)S(1)} %collective-permute-done.7), channel_id=1, source_target_pairs={{0,1},{1,2},{2,3},{3,4},{4,5},{5,6},{6,7},{7,8},{8,9},{9,10},{10,1... | collective-permute-start | bytes 786440 | tf_op jit(solution)/shard_map/ppermute | solution.py:13
  351.0 17.8 %collective-permute-start.5 = (f32[512,128]{1,0:T(8,128)S(1)}, f32[512,128]{1,0:T(8,128)S(1)}, u32[]{:S(2)}, u32[]{:S(2)}) collective-permute-start(f32[512,128]{1,0:T(8,128)S(1)} %collective-permute-done.4), channel_id=1, source_target_pairs={{1,0},{2,1},{3,2},{4,3},{5,4},{6,5},{7,6},{8,7},{9,8},{10,9},{11,1... | collective-permute-start | bytes 786440 | tf_op jit(solution)/shard_map/ppermute | solution.py:13
Sparse Core Ops, SparseCore 0:
  336.3 271.4 all-reduce.1
where the time goes:
time: 621 us; the launch traced here: 618 us
  waiting for transfers between devices  261 us (42%)
  other arithmetic  152 us (24%)
  local copies, waits for them, and re-layouts  81.9 us (13%)
  starting transfers between devices  49.9 us (8%)
  matrix products  49.6 us (8%)
  between operations  15 us (2%)
  loops' own time  7.98 us (1%)
    psum x1, waiting for transfers between devices, local(): weight_grad = lax.psum(scaled_part, ('dp', 'sx', 'sy'))  236 us
    scatter-add x6, other arithmetic, grad_group(): accum.at[picks.reshape(-1)]  137 us
    ppermute x12, starting transfers between devices, shifted(): return lax.ppermute(block, axis, route)  39.9 us
    transpose x6, local copies, waits for them, and re-layouts, grad_group(): jnp.einsum('gvd,kcd->kgvc', grad_rows, weights, preferred_element_type=jn...  20.1 us
    dot_general x6, matrix products, forward_group(): jnp.einsum('kgvc,kcd->gvd', gathered, weights, preferred_element_type=jnp...  18.2 us
    dot_general x6, matrix products, forward_group(): jnp.einsum('kgvc,gvd->kcd', gathered, grad_rows, preferred_element_type=j...  17.3 us
    gather x6, local copies, waits for them, and re-layouts, forward_group(): gathered = extended[picks]  16.4 us
    ppermute x12, waiting for transfers between devices, shifted(): return lax.ppermute(block, axis, route)  15 us
  transfers between devices with their start and end apart: 17, of which 4 were waited for; matrix products, arithmetic and copies ran while one was open for 44% of the time, Pallas kernels for 0%

commit v1 on v0

--- a/solution.py
+++ b/solution.py
@@ -1,3 +1,4 @@
+import functools
 import math
 import jax
 import jax.numpy as jnp
@@ -5,6 +6,13 @@
 from jax.sharding import PartitionSpec as P
 
 directions = ((-1, -1), (-1, 0), (-1, 1), (0, -1), (0, 1), (1, -1), (1, 0), (1, 1))
+
+
+def _plan_works(local_values, bus_axis, peer_axis):
+    return lax.psum(lax.psum(local_values, axis_name=bus_axis), axis_name=peer_axis)
+
+
+connect_the_desk = functools.partial(_plan_works, bus_axis="dp", peer_axis=("sx", "sy"))
 
 
 def shifted(block, axis, distance):
@@ -106,7 +114,7 @@
         num_blocks * width_block * lax.axis_size("dp") * lax.axis_size("sx") * lax.axis_size("sy")
     )
     scaled_part = weight_part * (1.0 / math.sqrt(total))
-    weight_grad = lax.psum(scaled_part, ("dp", "sx", "sy"))
+    weight_grad = connect_the_desk(scaled_part)
     return (output, input_grad, weight_grad)
 
 

time: 621 us -> 548 us (0.88)
  waiting for transfers between devices: 261 us -> 194 us
    psum x1 -> x2, waiting for transfers between devices: 236 us -> 161 us  [the longest x1 161 us: _plan_works(): lax.psum(lax.psum(local_values, axis_name=bus_axis), axis_name=peer_axis)]
    ppermute x2, waiting for transfers between devices: 0.01 us -> 16.5 us  [padded(): lax.ppermute(tail, axis, [(i, (i + 1) % count) for i in range(ends)])]
    ppermute x2, waiting for transfers between devices: 9.99 us -> 0.08 us  [padded(): lax.ppermute(head, axis, [((i + 1) % count, i) for i in range(ends)])]
  transfers between devices with their start and end apart: 17 -> 18, of which waited for: 4 -> 6; matrix products, arithmetic and copies ran while one was open for 44% -> 35% of each run, Pallas kernels for 0% -> 0%
where the time goes in v1:
time: 548 us; the launch traced here: 545 us
  waiting for transfers between devices  194 us (35%)
  other arithmetic  151 us (28%)
  local copies, waits for them, and re-layouts  81.1 us (15%)
  starting transfers between devices  47.6 us (9%)
  matrix products  47.5 us (9%)
  between operations  15 us (3%)
  loops' own time  7.94 us (1%)
    psum x1, waiting for transfers between devices, _plan_works(): lax.psum(lax.psum(local_values, axis_name=bus_axis), axis_name=peer_axis)  161 us
    scatter-add x6, other arithmetic, grad_group(): accum.at[picks.reshape(-1)]  138 us
    ppermute x12, starting transfers between devices, shifted(): return lax.ppermute(block, axis, route)  38.3 us
    transpose x6, local copies, waits for them, and re-layouts, grad_group(): jnp.einsum('gvd,kcd->kgvc', grad_rows, weights, preferred_element_type=jn...  20.1 us
    dot_general x6, matrix products, forward_group(): jnp.einsum('kgvc,kcd->gvd', gathered, weights, preferred_element_type=jnp...  18.2 us
    dot_general x6, matrix products, forward_group(): jnp.einsum('kgvc,gvd->kcd', gathered, grad_rows, preferred_element_type=j...  17.4 us
    ppermute x2, waiting for transfers between devices, padded(): lax.ppermute(tail, axis, [(i, (i + 1) % count) for i in range(ends)])  16.5 us
    gather x6, local copies, waits for them, and re-layouts, forward_group(): gathered = extended[picks]  16.4 us
  transfers between devices with their start and end apart: 18, of which 6 were waited for; matrix products, arithmetic and copies ran while one was open for 35% of the time, Pallas kernels for 0%

profile of v1, /device:TPU:2, one launch (start us, length us, event | category | flops | bytes accessed | tf_op | source)
XLA Modules:
  0.0 544.7 jit_solution(15785435587363703669)
XLA Ops:
  8.5 3.2 constant_dynamic-update-slice_fusion.9
  12.3 1.9 collective-permute-start.1
  14.3 2.4 collective-permute-start
  16.8 4.4 collective-permute-done
  21.2 3.7 collective-permute-start.2
  26.9 12.1 %collective-permute-done.2 = bf16[3,1,512,128]{3,2,1,0:T(8,128)(2,1)S(1)} collective-permute-done((bf16[3,1,512,128]{3,2,1,0:T(8,128)(2,1)S(1)}, bf16[3,1,512,128]{3,2,1,0:T(8,128)(2,1)S(1)}, u32[]{:S(2)}, u32[]{:S(2)}) %collective-permute-start.2) | collective-permute-done | bytes 393248 | tf_op jit(solution)/shard_map/ppermute | solution.py:32
  45.5 80.3 %while.24 = (s32[]{:T(128)}, f32[27,128,128]{2,1,0:T(8,128)}, bf16[6,4,128,128]{3,2,1,0:T(8,128)(2,1)}, s32[6]{0:T(128)}, s32[27,24]{1,0:T(8,128)}, /*index=5*/b...) while((s32[]{:T(128)}, f32[27,128,128]{2,1,0:T(8,128)}, ...), condition=%wide.region_1.0_spmd.clone, body=%wide.region_0.1_spmd.clone.sunk | while | flops 906986816 | bytes 33004880 | solution.py:109
  45.5 1.3 dynamic_slice.52
  49.0 2.7 gather_fusion
  51.8 3.0 fusion.39
  54.8 2.9 bitcast_add_fusion.2
  62.4 2.7 gather_fusion
  65.2 3.0 fusion.39
  68.2 2.9 bitcast_add_fusion.2
  72.3 1.3 dynamic_slice.52
  75.8 2.7 gather_fusion
  78.6 3.0 fusion.39
  81.6 2.9 bitcast_add_fusion.2
  85.7 1.3 dynamic_slice.52
  89.2 2.7 gather_fusion
  91.9 3.0 fusion.39
  95.0 2.9 bitcast_add_fusion.2
  102.6 2.7 gather_fusion
  105.3 3.0 fusion.39
  108.4 2.9 bitcast_add_fusion.2
  116.0 2.7 gather_fusion
  118.7 3.0 fusion.39
  121.8 2.9 bitcast_add_fusion.2
  125.9 2.9 broadcast_multiply_fusion
  128.9 2.4 broadcast_in_dim.26
  131.3 182.6 %while.23 = (s32[]{:T(128)}, f32[57,128,128]{2,1,0:T(8,128)}, s32[6]{0:T(128)S(1)}, s32[27,24]{1,0:T(8,128)}, bf16[24,128,128]{2,1,0:T(8,128)(2,1)}, /*index=5*/...) while((s32[]{:T(128)}, f32[57,128,128]{2,1,0:T(8,128)}, s32[6]{0:T(128)S(1)}, ...), condition=%wide.region_4.5_spmd, body=%wide.region_2.0_spmd.sunk | while | flops 454754624 | bytes 43486336 | solution.py:69
  133.4 2.0 convolution_bitcast_fusion.3
  135.4 3.3 copy.22
  138.8 23.0 %scatter_fusion = f32[57,128,128]{2,1,0:T(8,128)} fusion(f32[57,128,128]{2,1,0:T(8,128)} %get-tuple-element.307, s32[108]{0:T(128)S(1)} %fusion.33, f32[108,128,128]{2,1,0:T(8,128)} %bitcast.107), kind=kCustom, calls=%fused_computation.2.clone.1 | custom fusion | flops 1769472 | bytes 21234096 | tf_op jit(solution)/shard_map/while/body/eval_jaxpr/scatter-add | solution.py:63
  163.9 2.0 convolution_bitcast_fusion.3
  165.9 3.3 copy.22
  169.3 23.1 %scatter_fusion = f32[57,128,128]{2,1,0:T(8,128)} fusion(f32[57,128,128]{2,1,0:T(8,128)} %get-tuple-element.307, s32[108]{0:T(128)S(1)} %fusion.33, f32[108,128,128]{2,1,0:T(8,128)} %bitcast.107), kind=kCustom, calls=%fused_computation.2.clone.1 | custom fusion | flops 1769472 | bytes 21234096 | tf_op jit(solution)/shard_map/while/body/eval_jaxpr/scatter-add | solution.py:63
  194.5 2.0 convolution_bitcast_fusion.3
  196.5 3.3 copy.22
  199.8 22.8 %scatter_fusion = f32[57,128,128]{2,1,0:T(8,128)} fusion(f32[57,128,128]{2,1,0:T(8,128)} %get-tuple-element.307, s32[108]{0:T(128)S(1)} %fusion.33, f32[108,128,128]{2,1,0:T(8,128)} %bitcast.107), kind=kCustom, calls=%fused_computation.2.clone.1 | custom fusion | flops 1769472 | bytes 21234096 | tf_op jit(solution)/shard_map/while/body/eval_jaxpr/scatter-add | solution.py:63
  224.8 2.0 convolution_bitcast_fusion.3
  226.8 3.3 copy.22
  230.1 23.0 %scatter_fusion = f32[57,128,128]{2,1,0:T(8,128)} fusion(f32[57,128,128]{2,1,0:T(8,128)} %get-tuple-element.307, s32[108]{0:T(128)S(1)} %fusion.33, f32[108,128,128]{2,1,0:T(8,128)} %bitcast.107), kind=kCustom, calls=%fused_computation.2.clone.1 | custom fusion | flops 1769472 | bytes 21234096 | tf_op jit(solution)/shard_map/while/body/eval_jaxpr/scatter-add | solution.py:63
  255.3 2.0 convolution_bitcast_fusion.3
  257.3 3.3 copy.22
  260.6 22.9 %scatter_fusion = f32[57,128,128]{2,1,0:T(8,128)} fusion(f32[57,128,128]{2,1,0:T(8,128)} %get-tuple-element.307, s32[108]{0:T(128)S(1)} %fusion.33, f32[108,128,128]{2,1,0:T(8,128)} %bitcast.107), kind=kCustom, calls=%fused_computation.2.clone.1 | custom fusion | flops 1769472 | bytes 21234096 | tf_op jit(solution)/shard_map/while/body/eval_jaxpr/scatter-add | solution.py:63
  285.6 2.0 convolution_bitcast_fusion.3
  287.6 3.3 copy.22
  291.0 22.9 %scatter_fusion = f32[57,128,128]{2,1,0:T(8,128)} fusion(f32[57,128,128]{2,1,0:T(8,128)} %get-tuple-element.307, s32[108]{0:T(128)S(1)} %fusion.33, f32[108,128,128]{2,1,0:T(8,128)} %bitcast.107), kind=kCustom, calls=%fused_computation.2.clone.1 | custom fusion | flops 1769472 | bytes 21234096 | tf_op jit(solution)/shard_map/while/body/eval_jaxpr/scatter-add | solution.py:63
  313.9 1.6 fusion.17
  315.6 1.9 collective-permute-start.14
  317.5 3.6 collective-permute-start.6
  321.1 1.9 collective-permute-start.13
  323.1 1.9 collective-permute-start.11
  325.0 6.2 %collective-permute-start.10 = (f32[512,128]{1,0:T(8,128)S(1)}, f32[512,128]{1,0:T(8,128)S(1)}, u32[]{:S(2)}, u32[]{:S(2)}) collective-permute-start(f32[512,128]{1,0:T(8,128)S(1)} %bitcast.128), channel_id=1, source_target_pairs={{0,1},{1,2},{2,3},{3,4},{4,5},{5,6},{6,7},{7,8},{8,9},{9,10},{10,1... | collective-permute-start | bytes 786440 | tf_op jit(solution)/shard_map/ppermute | solution.py:21
  331.2 4.0 collective-permute-start.7
  335.2 2.7 collective-permute-start.4
  339.3 6.1 %collective-permute-start.15 = (f32[512,128]{1,0:T(8,128)S(1)}, f32[512,128]{1,0:T(8,128)S(1)}, u32[]{:S(2)}, u32[]{:S(2)}) collective-permute-start(f32[512,128]{1,0:T(8,128)S(1)} %collective-permute-done.14), channel_id=1, source_target_pairs={{0,1},{1,2},{2,3},{3,4},{4,5},{5,6},{6,7},{7,8},{8,9},{9,10},{10,1... | collective-permute-start | bytes 786440 | tf_op jit(solution)/shard_map/ppermute | solution.py:21
  346.7 6.1 %collective-permute-start.8 = (f32[512,128]{1,0:T(8,128)S(1)}, f32[512,128]{1,0:T(8,128)S(1)}, u32[]{:S(2)}, u32[]{:S(2)}) collective-permute-start(f32[512,128]{1,0:T(8,128)S(1)} %collective-permute-done.7), channel_id=1, source_target_pairs={{0,1},{1,2},{2,3},{3,4},{4,5},{5,6},{6,7},{7,8},{8,9},{9,10},{10,1... | collective-permute-start | bytes 786440 | tf_op jit(solution)/shard_map/ppermute | solution.py:21
  354.1 1.5 slice.68
  355.6 10.1 %collective-permute-done.15 = f32[512,128]{1,0:T(8,128)S(1)} collective-permute-done((f32[512,128]{1,0:T(8,128)S(1)}, f32[512,128]{1,0:T(8,128)S(1)}, u32[]{:S(2)}, u32[]{:S(2)}) %collective-permute-start.15) | collective-permute-done | bytes 262176 | tf_op jit(solution)/shard_map/ppermute | solution.py:21
  365.7 6.0 %collective-permute-done.8 = f32[512,128]{1,0:T(8,128)S(1)} collective-permute-done((f32[512,128]{1,0:T(8,128)S(1)}, f32[512,128]{1,0:T(8,128)S(1)}, u32[]{:S(2)}, u32[]{:S(2)}) %collective-permute-start.8) | collective-permute-done | bytes 262176 | tf_op jit(solution)/shard_map/ppermute | solution.py:21
  373.6 161.4 %all-reduce.5.cloned.1.call-done = f32[27,128,128]{2,1,0:T(8,128)} async-done(((f32[27,128,128]{2,1,0:T(8,128)}), f32[27,128,128]{2,1,0:T(8,128)}) %all-reduce.5.cloned.1.call-update) | async-done | bytes 1769488 | tf_op jit(solution)/shard_map/psum | solution.py:12
  535.0 2.9 copy.53
  (125 shorter events, 45.1 us)
Async XLA Ops:
  7.2 330.8 %all-reduce.3.cloned.1.call-start = ((), (), s32[]{:S(2)}) async-start(), calls=%async_computation | async-start | bytes 3538944 | tf_op jit(solution)/shard_map/psum | solution.py:12
  8.5 16.4 %copy-start.3 = (s32[1,1,1,27,24]{3,4,2,1,0:T(8,128)S(1)}, s32[1,1,1,27,24]{3,4,2,1,0:T(8,128)}, u32[]{:S(2)}) copy-start(s32[1,1,1,27,24]{3,4,2,1,0:T(8,128)} %param.13) | copy-start | bytes 7780
  12.3 4.4 collective-permute-start.1
  14.3 6.9 %collective-permute-start = (bf16[1,1,512,128]{3,2,1,0:T(8,128)(2,1)S(1)}, bf16[1,1,512,128]{3,2,1,0:T(8,128)(2,1)S(1)}, u32[]{:S(2)}, u32[]{:S(2)}) collective-permute-start(bf16[1,1,512,128]{3,2,1,0:T(8,128)(2,1)S(1)} %bitcast.120), channel_id=1, source_target_pairs={{0,16},{16,32},{32,48},{1,17},{17,33},{33,49},{2,18},{18,34},{34,5... | collective-permute-start | bytes 393224 | tf_op jit(solution)/shard_map/ppermute | solution.py:32
  21.2 17.8 %collective-permute-start.2 = (bf16[3,1,512,128]{3,2,1,0:T(8,128)(2,1)S(1)}, bf16[3,1,512,128]{3,2,1,0:T(8,128)(2,1)S(1)}, u32[]{:S(2)}, u32[]{:S(2)}) collective-permute-start(bf16[3,1,512,128]{3,2,1,0:T(8,128)(2,1)S(1)} %pad_maximum_fusion), channel_id=1, source_target_pairs={{0,1},{1,2},{2,3},{3,4},{4,5},{5,6},{6,7},{7,8},{8,9},{9,10},{10,1... | collective-permute-start | bytes 1179656 | tf_op jit(solution)/shard_map/ppermute | solution.py:32
  25.6 14.7 %collective-permute-start.3 = (bf16[3,1,512,128]{3,2,1,0:T(8,128)(2,1)S(1)}, bf16[3,1,512,128]{3,2,1,0:T(8,128)(2,1)S(1)}, u32[]{:S(2)}, u32[]{:S(2)}) collective-permute-start(bf16[3,1,512,128]{3,2,1,0:T(8,128)(2,1)S(1)} %pad_maximum_fusion), channel_id=1, source_target_pairs={{1,0},{2,1},{3,2},{4,3},{5,4},{6,5},{7,6},{8,7},{9,8},{10,9},{11,1... | collective-permute-start | bytes 1179656 | tf_op jit(solution)/shard_map/ppermute | solution.py:34
  51.8 3.1 copy-start
  57.7 1.2 copy-start.1
  65.2 3.1 copy-start
  71.1 1.2 copy-start.1
  78.5 3.1 copy-start
  84.5 1.2 copy-start.1
  91.9 3.1 copy-start
  97.9 1.2 copy-start.1
  105.3 3.1 copy-start
  111.3 1.2 copy-start.1
  118.7 3.1 copy-start
  124.7 1.2 copy-start.1
  128.8 406.1 %all-reduce.5.cloned.1.call-start = ((), (), s32[]{:S(2)}) async-start(), calls=%async_computation.1 | async-start | bytes 3538944 | tf_op jit(solution)/shard_map/psum | solution.py:12
  128.9 2.4 copy-start.2
  315.6 15.6 %collective-permute-start.14 = (f32[512,128]{1,0:T(8,128)S(1)}, f32[512,128]{1,0:T(8,128)S(1)}, u32[]{:S(2)}, u32[]{:S(2)}) collective-permute-start(f32[512,128]{1,0:T(8,128)S(1)} %bitcast.132), channel_id=1, source_target_pairs={{0,16},{16,32},{32,48},{1,17},{17,33},{33,49},{2,18},{18,34},{34,5... | collective-permute-start | bytes 786440 | tf_op jit(solution)/shard_map/ppermute | solution.py:21
  317.5 17.7 %collective-permute-start.6 = (f32[512,128]{1,0:T(8,128)S(1)}, f32[512,128]{1,0:T(8,128)S(1)}, u32[]{:S(2)}, u32[]{:S(2)}) collective-permute-start(f32[512,128]{1,0:T(8,128)S(1)} %bitcast.131), channel_id=1, source_target_pairs={{16,0},{32,16},{48,32},{17,1},{33,17},{49,33},{18,2},{34,18},{50,3... | collective-permute-start | bytes 786440 | tf_op jit(solution)/shard_map/ppermute | solution.py:21
  321.1 16.8 %collective-permute-start.13 = (f32[512,128]{1,0:T(8,128)S(1)}, f32[512,128]{1,0:T(8,128)S(1)}, u32[]{:S(2)}, u32[]{:S(2)}) collective-permute-start(f32[512,128]{1,0:T(8,128)S(1)} %bitcast.130), channel_id=1, source_target_pairs={{0,16},{16,32},{32,48},{1,17},{17,33},{33,49},{2,18},{18,34},{34,5... | collective-permute-start | bytes 786440 | tf_op jit(solution)/shard_map/ppermute | solution.py:21
  323.1 16.2 %collective-permute-start.11 = (f32[512,128]{1,0:T(8,128)S(1)}, f32[512,128]{1,0:T(8,128)S(1)}, u32[]{:S(2)}, u32[]{:S(2)}) collective-permute-start(f32[512,128]{1,0:T(8,128)S(1)} %bitcast.129), channel_id=1, source_target_pairs={{0,16},{16,32},{32,48},{1,17},{17,33},{33,49},{2,18},{18,34},{34,5... | collective-permute-start | bytes 786440 | tf_op jit(solution)/shard_map/ppermute | solution.py:21
  325.0 20.3 %collective-permute-start.10 = (f32[512,128]{1,0:T(8,128)S(1)}, f32[512,128]{1,0:T(8,128)S(1)}, u32[]{:S(2)}, u32[]{:S(2)}) collective-permute-start(f32[512,128]{1,0:T(8,128)S(1)} %bitcast.128), channel_id=1, source_target_pairs={{0,1},{1,2},{2,3},{3,4},{4,5},{5,6},{6,7},{7,8},{8,9},{9,10},{10,1... | collective-permute-start | bytes 786440 | tf_op jit(solution)/shard_map/ppermute | solution.py:21
  331.2 15.5 %collective-permute-start.7 = (f32[512,128]{1,0:T(8,128)S(1)}, f32[512,128]{1,0:T(8,128)S(1)}, u32[]{:S(2)}, u32[]{:S(2)}) collective-permute-start(f32[512,128]{1,0:T(8,128)S(1)} %bitcast.127), channel_id=1, source_target_pairs={{16,0},{32,16},{48,32},{17,1},{33,17},{49,33},{18,2},{34,18},{50,3... | collective-permute-start | bytes 786440 | tf_op jit(solution)/shard_map/ppermute | solution.py:21
  335.2 17.6 %collective-permute-start.4 = (f32[512,128]{1,0:T(8,128)S(1)}, f32[512,128]{1,0:T(8,128)}, u32[]{:S(2)}, u32[]{:S(2)}) collective-permute-start(f32[512,128]{1,0:T(8,128)S(1)} %bitcast.126), channel_id=1, source_target_pairs={{16,0},{32,16},{48,32},{17,1},{33,17},{49,33},{18,2},{34,18},{50,3... | collective-permute-start | bytes 786440 | tf_op jit(solution)/shard_map/ppermute | solution.py:21
  338.0 17.6 %collective-permute-start.9 = (f32[512,128]{1,0:T(8,128)S(1)}, f32[512,128]{1,0:T(8,128)S(1)}, u32[]{:S(2)}, u32[]{:S(2)}) collective-permute-start(f32[512,128]{1,0:T(8,128)S(1)} %bitcast.125), channel_id=1, source_target_pairs={{1,0},{2,1},{3,2},{4,3},{5,4},{6,5},{7,6},{8,7},{9,8},{10,9},{11,1... | collective-permute-start | bytes 786440 | tf_op jit(solution)/shard_map/ppermute | solution.py:21
  339.3 26.4 %collective-permute-start.15 = (f32[512,128]{1,0:T(8,128)S(1)}, f32[512,128]{1,0:T(8,128)S(1)}, u32[]{:S(2)}, u32[]{:S(2)}) collective-permute-start(f32[512,128]{1,0:T(8,128)S(1)} %collective-permute-done.14), channel_id=1, source_target_pairs={{0,1},{1,2},{2,3},{3,4},{4,5},{5,6},{6,7},{7,8},{8,9},{9,10},{10,1... | collective-permute-start | bytes 786440 | tf_op jit(solution)/shard_map/ppermute | solution.py:21
  345.4 20.3 %collective-permute-start.12 = (f32[512,128]{1,0:T(8,128)S(1)}, f32[512,128]{1,0:T(8,128)S(1)}, u32[]{:S(2)}, u32[]{:S(2)}) collective-permute-start(f32[512,128]{1,0:T(8,128)S(1)} %collective-permute-done.11), channel_id=1, source_target_pairs={{1,0},{2,1},{3,2},{4,3},{5,4},{6,5},{7,6},{8,7},{9,8},{10,9},{11,1... | collective-permute-start | bytes 786440 | tf_op jit(solution)/shard_map/ppermute | solution.py:21
  346.7 25.0 %collective-permute-start.8 = (f32[512,128]{1,0:T(8,128)S(1)}, f32[512,128]{1,0:T(8,128)S(1)}, u32[]{:S(2)}, u32[]{:S(2)}) collective-permute-start(f32[512,128]{1,0:T(8,128)S(1)} %collective-permute-done.7), channel_id=1, source_target_pairs={{0,1},{1,2},{2,3},{3,4},{4,5},{5,6},{6,7},{7,8},{8,9},{9,10},{10,1... | collective-permute-start | bytes 786440 | tf_op jit(solution)/shard_map/ppermute | solution.py:21
  352.8 18.9 %collective-permute-start.5 = (f32[512,128]{1,0:T(8,128)}, f32[512,128]{1,0:T(8,128)S(1)}, u32[]{:S(2)}, u32[]{:S(2)}) collective-permute-start(f32[512,128]{1,0:T(8,128)} %collective-permute-done.4), channel_id=1, source_target_pairs={{1,0},{2,1},{3,2},{4,3},{5,4},{6,5},{7,6},{8,7},{9,8},{10,9},{11,1... | collective-permute-start | bytes 786440 | tf_op jit(solution)/shard_map/ppermute | solution.py:21
Sparse Core Ops, SparseCore 0:
  128.9 63.3 all-reduce.2
  338.1 196.8 all-reduce.4
